TPU v7x, 32 devices: a whole 2x2x4 slice. The times are simulated.
32 devices in a mesh: parts: 2 (over x), chol: 16 (over z, y, core).
Axes of the slice: x: 2, y: 2, z: 4, core: 2. Of those that a mesh axis runs over, the one named last changes fastest.
Arguments:
- orbitals: float32 [32, 100, 1024], P(('parts', 'chol')), parts along dimension 0, may hold values from -6 to 6
- intersection_inv: float32 [32, 100, 100], P(('parts', 'chol')), parts along dimension 0, may hold values from -0.625 to 0.625
- factor_rows: bfloat16 [4096, 1024], P('chol'), may hold values from -0.1875 to 0.1875
- factor_rotated: bfloat16 [100, 4096], replicated, may hold values from -0.625 to 0.625
- factor_core: bfloat16 [1024, 4096], P('chol'), may hold values from -0.125 to 0.125
- fields: float32 [32, 1024], P('parts', 'chol'), parts along dimension 0, may hold values from -6 to 6
Outputs:
- propagated: float32 [32, 100, 1024], P(('parts', 'chol')), parts along dimension 0
- force_bias: float32 [32, 1024], P('parts', 'chol'), parts along dimension 0
There are 2 independent parts, one for each index of `parts`. A program takes and returns all parts, laid end to end along the dimension named above; an argument that names none is the same for every part. Nothing has to cross between parts.
All inputs are finite; a program needn't handle non-finite values.
Results may differ from a plain program's by a relative error of at most 0.0091.
Values may be sent and summed in bfloat16 or wider, within the bound.
A program may use at most 64 MiB of HBM per device.

v0:
```python
import jax
import jax.numpy as jnp
from jax import lax
from jax.sharding import PartitionSpec as P

TAYLOR = 4


def density_one(half_green, all_rows, factor_rotated):
    projected = lax.dot_general(
        half_green, all_rows, (((1,), (1,)), ((), ())), preferred_element_type=jnp.float32
    )
    return jnp.sum(factor_rotated.astype(jnp.float32) * projected, axis=0).astype(jnp.bfloat16)


def propagate_one(orbital, potential, all_rows):
    total = orbital
    term = orbital
    for order in range(1, TAYLOR + 1):
        summed = lax.dot_general(
            term.astype(jnp.bfloat16),
            all_rows,
            (((1,), (1,)), ((), ())),
            preferred_element_type=jnp.float32,
        )
        scaled = (summed * potential[None, :] / order).astype(jnp.bfloat16)
        term = jnp.dot(scaled, all_rows, preferred_element_type=jnp.float32)
        total = total + term
    return total


def on_device(orbitals, intersection_inv, factor_rows, factor_rotated, factor_core, fields):
    walker_count = orbitals.shape[0]
    half_green = jnp.einsum(
        "wij,wjm->wim", intersection_inv, orbitals, precision=lax.Precision.HIGHEST
    ).astype(jnp.bfloat16)
    all_rows = lax.all_gather(factor_rows, "chol", axis=0, tiled=True)
    own_density = lax.map(lambda item: density_one(item, all_rows, factor_rotated), half_green)
    density = lax.all_gather(own_density, "chol", axis=0, tiled=True)
    force_bias = lax.dot_general(
        density, factor_core, (((1,), (1,)), ((), ())), preferred_element_type=jnp.float32
    )
    shifted = (fields - force_bias).astype(jnp.bfloat16)
    partial_sum = jnp.dot(shifted, factor_core, preferred_element_type=jnp.float32)
    summed_all = lax.psum(partial_sum, "chol")
    potential = lax.dynamic_slice_in_dim(
        summed_all, lax.axis_index("chol") * walker_count, walker_count, 0
    )
    propagated = lax.map(
        lambda pair: propagate_one(pair[0], pair[1], all_rows), (orbitals, potential)
    )
    return (propagated, force_bias)


def solution(mesh):
    in_specs = (
        P(("parts", "chol"), None, None),
        P(("parts", "chol"), None, None),
        P("chol", None),
        P(),
        P("chol", None),
        P("parts", "chol"),
    )
    out_specs = (P(("parts", "chol"), None, None), P("parts", "chol"))
    return jax.shard_map(
        on_device, mesh=mesh, in_specs=in_specs, out_specs=out_specs, check_vma=False
    )
```

profile of v0, /device:TPU:0, one launch (start us, length us, event | category | flops | bytes accessed | tf_op | source)
XLA Modules:
  0.0 249.2 jit_solution(8666170632495442712)
XLA Ops:
  7.2 0.0 copy-start
  7.2 0.0 copy-start.1
  7.2 0.0 copy-start.3
  7.2 0.0 all-gather.3.cloned.1.call-start
  7.2 0.7 all-gather.3.cloned.1.call-update
  7.9 0.0 all-reduce.2.cloned.1.call-start
  8.0 1.6 convolution_convert_fusion
  9.6 77.7 %all-gather.3.cloned.1.call-done = bf16[4096,1024]{1,0:T(8,128)(2,1)} async-done(((bf16[256,1024]{1,0:T(8,128)(2,1)}), bf16[4096,1024]{1,0:T(8,128)(2,1)}) %all-gather.3.cloned.1.call-update) | async-done | bytes 8388624 | tf_op jit(solution)/shard_map/all_gather | solution.py:37
  87.2 6.3 %fusion.7 = bf16[4096]{0:T(1024)(128)(2,1)S(1)} fusion(bf16[100,1024]{1,0:T(8,128)(2,1)S(1)} %convolution_convert_fusion, bf16[4096,1024]{1,0:T(8,128)(2,1)} %all-gather.3.cloned.1.call-done, bf16[100,4096]{1,0:T(8,128)(2,1)} %param.9), kind=kOutput, calls=%fused_computation.12 | convolution fusion | flops 840085504 | bytes 9420800 | tf_op jit(solution)/shard_map/while/body/eval_jaxpr/dot_general | solution.py:10
  93.5 19.5 %all-gather = bf16[65536]{0:T(1024)(128)(2,1)S(1)} all-gather(bf16[4096]{0:T(1024)(128)(2,1)S(1)} %fusion.7), channel_id=2, replica_groups=mesh['parts'=2,'chol'=16] {'chol'}, dimensions={0}, use_global_device_ids=true | all-gather | bytes 139264 | tf_op jit(solution)/shard_map/all_gather | solution.py:39
  113.0 0.1 reshape.20
  113.1 0.0 copy-done
  113.1 0.2 fusion.28
  113.3 0.0 copy-done.3
  113.3 0.0 copy-start.2
  113.3 0.9 fusion.24
  114.2 0.0 all-reduce.2.cloned.1.call-update
  114.3 87.1 %all-reduce.2.cloned.1.call-done = f32[16,4096]{1,0:T(8,128)} async-done(((f32[16,4096]{1,0:T(8,128)}), f32[16,4096]{1,0:T(8,128)}) %all-reduce.2.cloned.1.call-update) | async-done | bytes 262160 | tf_op jit(solution)/shard_map/psum | solution.py:45
  201.4 0.9 constant_dynamic-slice_fusion
  202.3 0.0 copy-done.1
  202.3 9.7 %fusion.11 = f32[100,1024]{1,0:T(8,128)S(1)} fusion(bf16[4096,1024]{1,0:T(8,128)(2,1)} %all-gather.3.cloned.1.call-done, f32[4096]{0:T(1024)S(1)} %bitcast.32, f32[1,100,1024]{2,0,1:T(1,128)S(1)} %copy-done.1), kind=kOutput, calls=%fused_computation.18 | convolution fusion | flops 1678540800 | bytes 9224192 | tf_op jit(solution)/shard_map/while/body/eval_jaxpr/dot_general | solution.py:27
  212.0 0.0 copy-done.2
  212.0 9.7 %fusion.10 = f32[100,1024]{1,0:T(8,128)S(1)} fusion(bf16[4096,1024]{1,0:T(8,128)(2,1)} %all-gather.3.cloned.1.call-done, f32[4096]{0:T(1024)S(1)} %bitcast.33, f32[100,1024]{1,0:T(8,128)S(1)} %fusion.11), kind=kOutput, calls=%fused_computation.17 | convolution fusion | flops 1679052800 | bytes 9224192 | tf_op jit(solution)/shard_map/while/body/eval_jaxpr/dot_general | solution.py:27
  221.7 9.7 %fusion.9 = f32[100,1024]{1,0:T(8,128)S(1)} fusion(bf16[4096,1024]{1,0:T(8,128)(2,1)} %all-gather.3.cloned.1.call-done, f32[4096]{0:T(1024)S(1)} %bitcast.34, f32[100,1024]{1,0:T(8,128)S(1)} %fusion.10), kind=kOutput, calls=%fused_computation.16 | convolution fusion | flops 1679052800 | bytes 9224192 | tf_op jit(solution)/shard_map/while/body/eval_jaxpr/dot_general | solution.py:27
  231.5 9.7 %fusion.8 = f32[1,100,1024]{2,1,0:T(8,128)S(1)} fusion(bf16[4096,1024]{1,0:T(8,128)(2,1)} %all-gather.3.cloned.1.call-done, f32[4096]{0:T(1024)S(1)} %bitcast.35, f32[100,1024]{1,0:T(8,128)S(1)} %fusion.9, f32[100,1024]{1,0:T(8,128)S(1)} %fusion.10, f32[100,1024]{1,0:T(8,128)S(1)} %fusion.11, f32[1,100,1024]{2,0,1:T(1,128)S(1)} %copy-done.1), kind=kOutput, calls=%fused_computation.14 | convolution fusion | flops 1679462400 | bytes 10452992 | tf_op jit(solution)/shard_map/while/body/eval_jaxpr/dot_general | solution.py:27
  241.2 1.2 copy.9
Async XLA Ops:
  7.2 105.9 %copy-start = (bf16[64,4096]{1,0:T(8,128)(2,1)S(1)}, bf16[64,4096]{1,0:T(8,128)(2,1)}, u32[]{:S(2)}) copy-start(bf16[64,4096]{1,0:T(8,128)(2,1)} %param.10) | copy-start | bytes 1572868
  7.2 195.2 %copy-start.1 = (f32[1,100,1024]{2,0,1:T(1,128)S(1)}, f32[1,100,1024]{2,0,1:T(1,128)}, u32[]{:S(2)}) copy-start(f32[1,100,1024]{2,0,1:T(1,128)} %param.6) | copy-start | bytes 1228804
  7.2 106.1 %copy-start.3 = (f32[16,64]{1,0:T(8,128)S(1)}, f32[16,64]{1,0:T(8,128)}, u32[]{:S(2)}) copy-start(f32[16,64]{1,0:T(8,128)} %param.11) | copy-start | bytes 12292
  7.2 80.0 %all-gather.3.cloned.1.call-start = ((), (), s32[]{:S(2)}) async-start(), calls=%async_computation | async-start | bytes 8912896 | tf_op jit(solution)/shard_map/all_gather | solution.py:37
  7.9 193.5 %all-reduce.2.cloned.1.call-start = ((), (), s32[]{:S(2)}) async-start(), calls=%async_computation.1 | async-start | bytes 524288 | tf_op jit(solution)/shard_map/psum | solution.py:45
  113.3 98.7 %copy-start.2 = (f32[16,64]{1,0:T(8,128)}, f32[16,64]{1,0:T(8,128)S(1)}, u32[]{:S(2)}) copy-start(f32[16,64]{1,0:T(8,128)S(1)} %fusion.28) | copy-start | bytes 12292
Sparse Core Ops, SparseCore 0:
  10.2 77.0 all-gather.2
  114.4 86.9 all-reduce.1
where the time goes:
time: 249 us
  waiting for transfers between devices  166 us (67%)
  matrix products  47.9 us (19%)
  blocking collectives  19.5 us (8%)
  between operations  14.1 us (6%)
    psum x1, waiting for transfers between devices, on_device(): summed_all = lax.psum(partial_sum, 'chol')  87.1 us
    all_gather x1, waiting for transfers between devices, on_device(): all_rows = lax.all_gather(factor_rows, 'chol', axis=0, tiled=True)  77.7 us
    dot_general x4, matrix products, propagate_one(): term = jnp.dot(scaled, all_rows, preferred_element_type=jnp.float32)  38.9 us
    all_gather x1, blocking collectives, on_device(): density = lax.all_gather(own_density, 'chol', axis=0, tiled=True)  19.5 us
    dot_general x1, matrix products, density_one(): lax.dot_general(half_green, all_rows, (((1,), (1,)), ((), ())), preferred...  6.26 us
  transfers between devices with their start and end apart: 2, of which 2 were waited for; matrix products, arithmetic and copies ran while one was open for 1% of the time, Pallas kernels for 0%

commit v1 on v0

v1 whole, which is shorter than its diff:
```python
import functools

import jax
import jax.numpy as jnp
from jax import lax
from jax.experimental import pallas as pl
from jax.experimental.pallas import tpu as pltpu
from jax.sharding import PartitionSpec as P

TAYLOR = 4
F32, BF16 = jnp.float32, jnp.bfloat16
LAST = (((1,), (1,)), ((), ()))


def kernel(
    n, orb_ref, inv_ref, rows_ref, rot_ref, core_ref, fields_ref, out_ref, fb_ref,
    xbuf, lhs, pad, rot, corep, s1, sc, dbuf, dfull, pbuf, rbuf, pot, tpart, tsend, trecv, tbf, total,
    own_sem, rot_sem, core_sem, ring_send, ring_recv, pair_send, pair_recv,
    dens_send, dens_recv, pot_send, pot_recv, term_send, term_recv,
):
    h = n // 2
    p, m = rows_ref.shape
    ne = orb_ref.shape[1]
    nep = pad.shape[0]
    half = h * p
    piece = p // 2
    me = lax.axis_index("chol")
    q, c = me // 2, me % 2
    partner = q * 2 + (1 - c)
    r = (1 - q % 2) * (q // 2) + (q % 2) * (h - 1 - q // 2)

    def chip_at(pos):
        pos = (pos + 2 * h) % h
        s = pos // (h // 2)
        return (1 - s) * 2 * pos + s * (2 * (h - 1 - pos) + 1)

    barrier = pltpu.get_barrier_semaphore()
    for k in range(1, n):
        pl.semaphore_signal(barrier, inc=1, device_id={"chol": (me + k) % n}, device_id_type=pl.DeviceIdType.MESH)

    own_copy = pltpu.make_async_copy(rows_ref, xbuf.at[pl.ds(pl.multiple_of(q * p, p), p)], own_sem)
    own_copy.start()
    rot_copy = pltpu.make_async_copy(rot_ref, rot, rot_sem)
    rot_copy.start()
    core_copies = []
    for s in range(n):
        copy = pltpu.make_async_copy(
            core_ref.at[:, pl.ds(s * p, p)],
            corep.at[:, pl.ds((s % 2) * half + (s // 2) * p, p)],
            core_sem.at[s],
        )
        copy.start()
        core_copies.append(copy)

    pl.semaphore_wait(barrier, n - 1)

    def remote(src, dst, send, recv, target):
        return pltpu.make_async_remote_copy(
            src_ref=src, dst_ref=dst, send_sem=send, recv_sem=recv,
            device_id={"chol": target}, device_id_type=pl.DeviceIdType.MESH,
        )

    def slot(chip, part):
        return xbuf.at[pl.ds(pl.multiple_of(chip * p + part * piece, piece), piece)]

    def hop(way, step, part):
        sign = 1 - 2 * way
        origin = chip_at(r - sign * (step - 1))
        src = rows_ref.at[pl.ds(part * piece, piece)] if step == 1 else slot(origin, part)
        return remote(
            src, slot(origin, part), ring_send.at[way, step - 1, part], ring_recv.at[way, step - 1, part],
            chip_at(r + sign) * 2 + c,
        )

    def arrival(way, step, part):
        sign = 1 - 2 * way
        here = slot(chip_at(r - sign * step), part)
        return remote(
            here, here, ring_send.at[way, step - 1, part], ring_recv.at[way, step - 1, part], chip_at(r + sign) * 2 + c
        )

    def travels(way, step, part):
        return step < h // 2 or (step == h // 2 and part == way)

    sent = []
    for part in range(2):
        for way in range(2):
            if travels(way, 1, part):
                copy = hop(way, 1, part)
                copy.start()
                sent.append(copy)

    own_walker = orb_ref[0]
    pad[...] = jnp.zeros_like(pad)
    pad[0:ne] = own_walker
    total[...] = pad[...]
    lhs[c, nep : 2 * nep] = pad[...].astype(BF16)
    pad[0:ne] = jnp.dot(inv_ref[0], own_walker, preferred_element_type=F32, precision=lax.Precision.HIGHEST)
    lhs[c, 0:nep] = pad[...].astype(BF16)
    pair = remote(lhs.at[c], lhs.at[c], pair_send, pair_recv, partner)
    pair.start()
    sent.append(pair)
    own_copy.wait()
    rot_copy.wait()
    remote(lhs.at[1 - c], lhs.at[1 - c], pair_send, pair_recv, partner).wait_recv()

    def block(chip):
        where = pl.ds(pl.multiple_of(chip * p, p), p)
        result = lax.dot_general(
            lhs[...].reshape(4 * nep, m), xbuf[where, :], LAST, preferred_element_type=F32
        )
        rotated = rot[:, pl.ds(pl.multiple_of((chip * 2 + c) * p, p), p)].astype(F32)
        for w in range(2):
            projected = result[w * 2 * nep : w * 2 * nep + ne]
            density = jnp.sum(rotated * projected, axis=0, keepdims=True)
            dbuf[me, w : w + 1, where] = density.astype(BF16).astype(F32)
            s1[w * nep : (w + 1) * nep, where] = result[w * 2 * nep + nep : (w + 1) * 2 * nep]

    block(q)
    for step in range(1, h // 2 + 1):
        for part in range(2):
            for way in range(2):
                if travels(way, step, part):
                    arrival(way, step, part).wait_recv()
                    if travels(way, step + 1, part):
                        copy = hop(way, step + 1, part)
                        copy.start()
                        sent.append(copy)
        block(chip_at(r - step))
        if step < h // 2:
            block(chip_at(r + step))

    for k in range(1, n):
        copy = remote(dbuf.at[me], dbuf.at[me], dens_send.at[k - 1], dens_recv.at[k - 1], (me + k) % n)
        copy.start()
        sent.append(copy)
    for copy in core_copies:
        copy.wait()
    for k in range(1, n):
        source = (me + n - k) % n
        remote(dbuf.at[source], dbuf.at[source], dens_send.at[k - 1], dens_recv.at[k - 1], source).wait_recv()
    for s in range(n):
        dfull[2 * (s // 2) : 2 * (s // 2) + 2, (s % 2) * half : (s % 2 + 1) * half] = dbuf[s]
    force_bias = lax.dot_general(dfull[...].astype(BF16), corep[...], LAST, preferred_element_type=F32)
    fb_ref[...] = force_bias
    shifted = (fields_ref[...] - force_bias).astype(BF16)
    for side in range(2):
        dfull[:, side * half : (side + 1) * half] = jnp.dot(
            shifted, corep[:, side * half : (side + 1) * half], preferred_element_type=F32
        )
    for s in range(n):
        pbuf[s] = dfull[2 * (s // 2) : 2 * (s // 2) + 2, (s % 2) * half : (s % 2 + 1) * half]
    for k in range(1, n):
        target = (me + k) % n
        copy = remote(pbuf.at[target], rbuf.at[k - 1], pot_send.at[k - 1], pot_recv.at[k - 1], target)
        copy.start()
        sent.append(copy)
    summed = pbuf[me]
    for k in range(1, n):
        remote(rbuf.at[k - 1], rbuf.at[k - 1], pot_send.at[k - 1], pot_recv.at[k - 1], partner).wait_recv()
        summed = summed + rbuf[k - 1]
    pot[...] = summed

    wide = tpart.shape[2]
    for order in range(1, TAYLOR + 1):
        for j in range(h):
            where = slice(j * p, (j + 1) * p)
            if order == 1:
                result = s1[:, where]
            else:
                result = lax.dot_general(tbf[...], xbuf[where, :], LAST, preferred_element_type=F32)
            for w in range(2):
                scale = pot[w : w + 1, where] / order
                sc[w * nep : (w + 1) * nep, where] = (result[w * nep : (w + 1) * nep] * scale).astype(BF16)
        last = order == TAYLOR
        for j in range(m // wide):
            result = jnp.dot(sc[...], xbuf[:, j * wide : (j + 1) * wide], preferred_element_type=F32)
            tpart[j] = result
            tsend[order - 1, j] = result.astype(BF16)
            mine = pl.ds(pl.multiple_of((1 - c) * nep, nep), nep) if last else pl.ds(0, 2 * nep)
            view = (order - 1, j, mine)
            copy = remote(
                tsend.at[view], trecv.at[view], term_send.at[order - 1, j], term_recv.at[order - 1, j], partner
            )
            copy.start()
            sent.append(copy)
        own = pl.ds(pl.multiple_of(c * nep, nep), nep)
        for j in range(m // wide):
            where = slice(j * wide, (j + 1) * wide)
            mine = own if last else pl.ds(0, 2 * nep)
            view = trecv.at[order - 1, j, mine]
            remote(view, view, term_send.at[order - 1, j], term_recv.at[order - 1, j], partner).wait_recv()
            total[:, where] += tpart[j, own] + trecv[order - 1, j, own].astype(F32)
            if not last:
                tbf[:, where] = (tpart[j] + trecv[order - 1, j].astype(F32)).astype(BF16)
    out_ref[0] = total[0:ne]
    for copy in sent:
        copy.wait_send()


def fused(orbitals, intersection_inv, factor_rows, factor_rotated, factor_core, fields, n):
    h = n // 2
    p, m = factor_rows.shape
    ne, points = factor_rotated.shape
    nep = -(-ne // 16) * 16
    half = h * p
    walkers = fields.shape[0]
    wide = 256
    vmem = pl.BlockSpec(memory_space=pltpu.VMEM)
    hbm = pl.BlockSpec(memory_space=pl.ANY)
    dma = pltpu.SemaphoreType.DMA
    return pl.pallas_call(
        functools.partial(kernel, n),
        out_shape=(
            jax.ShapeDtypeStruct(orbitals.shape, F32),
            jax.ShapeDtypeStruct(fields.shape, F32),
        ),
        in_specs=[vmem, vmem, hbm, hbm, hbm, vmem],
        out_specs=(vmem, vmem),
        scratch_shapes=[
            pltpu.VMEM((half, m), BF16),
            pltpu.VMEM((2, 2 * nep, m), BF16),
            pltpu.VMEM((nep, m), F32),
            pltpu.VMEM((ne, points), BF16),
            pltpu.VMEM(factor_core.shape, BF16),
            pltpu.VMEM((2 * nep, half), F32),
            pltpu.VMEM((2 * nep, half), BF16),
            pltpu.VMEM((n, 2, half), F32),
            pltpu.VMEM((walkers, points), F32),
            pltpu.VMEM((n, 2, half), F32),
            pltpu.VMEM((n - 1, 2, half), F32),
            pltpu.VMEM((2, half), F32),
            pltpu.VMEM((m // wide, 2 * nep, wide), F32),
            pltpu.VMEM((TAYLOR, m // wide, 2 * nep, wide), BF16),
            pltpu.VMEM((TAYLOR, m // wide, 2 * nep, wide), BF16),
            pltpu.VMEM((2 * nep, m), BF16),
            pltpu.VMEM((nep, m), F32),
            dma(()),
            dma(()),
            dma((n,)),
            dma((2, h // 2, 2)),
            dma((2, h // 2, 2)),
            dma(()),
            dma(()),
            dma((n - 1,)),
            dma((n - 1,)),
            dma((n - 1,)),
            dma((n - 1,)),
            dma((TAYLOR, m // wide)),
            dma((TAYLOR, m // wide)),
        ],
        compiler_params=pltpu.CompilerParams(
            collective_id=0, has_side_effects=True, vmem_limit_bytes=56 * 1024 * 1024
        ),
    )(orbitals, intersection_inv, factor_rows, factor_rotated, factor_core, fields)


def density_one(half_green, all_rows, factor_rotated):
    projected = lax.dot_general(half_green, all_rows, LAST, preferred_element_type=F32)
    return jnp.sum(factor_rotated.astype(F32) * projected, axis=0).astype(BF16)


def propagate_one(orbital, potential, all_rows):
    total = orbital
    term = orbital
    for order in range(1, TAYLOR + 1):
        summed = lax.dot_general(term.astype(BF16), all_rows, LAST, preferred_element_type=F32)
        scaled = (summed * potential[None, :] / order).astype(BF16)
        term = jnp.dot(scaled, all_rows, preferred_element_type=F32)
        total = total + term
    return total


def plain(orbitals, intersection_inv, factor_rows, factor_rotated, factor_core, fields):
    walker_count = orbitals.shape[0]
    half_green = jnp.einsum(
        "wij,wjm->wim", intersection_inv, orbitals, precision=lax.Precision.HIGHEST
    ).astype(BF16)
    all_rows = lax.all_gather(factor_rows, "chol", axis=0, tiled=True)
    own_density = lax.map(lambda item: density_one(item, all_rows, factor_rotated), half_green)
    density = lax.all_gather(own_density, "chol", axis=0, tiled=True)
    force_bias = lax.dot_general(density, factor_core, LAST, preferred_element_type=F32)
    shifted = (fields - force_bias).astype(BF16)
    partial_sum = jnp.dot(shifted, factor_core, preferred_element_type=F32)
    summed_all = lax.psum(partial_sum, "chol")
    potential = lax.dynamic_slice_in_dim(
        summed_all, lax.axis_index("chol") * walker_count, walker_count, 0
    )
    propagated = lax.map(lambda pair: propagate_one(pair[0], pair[1], all_rows), (orbitals, potential))
    return (propagated, force_bias)


def solution(mesh):
    n = mesh.shape["chol"]

    def on_device(orbitals, intersection_inv, factor_rows, factor_rotated, factor_core, fields):
        args = (orbitals, intersection_inv, factor_rows, factor_rotated, factor_core, fields)
        rows, m = factor_rows.shape
        if orbitals.shape[0] == 1 and n % 4 == 0 and rows % 256 == 0 and m % 256 == 0:
            return fused(*args, n)
        return plain(*args)

    in_specs = (
        P(("parts", "chol"), None, None),
        P(("parts", "chol"), None, None),
        P("chol", None),
        P(),
        P("chol", None),
        P("parts", "chol"),
    )
    out_specs = (P(("parts", "chol"), None, None), P("parts", "chol"))
    return jax.shard_map(
        on_device, mesh=mesh, in_specs=in_specs, out_specs=out_specs, check_vma=False
    )
```

time: 249 us -> 89.5 us (0.36)
  waiting for transfers between devices: 166 us -> 0 us
  Pallas kernels: 0 us -> 82.6 us
  matrix products: 47.9 us -> 0 us
  blocking collectives: 19.5 us -> 0 us
  between operations: 14.1 us -> 0.65 us
  local copies, waits for them, and re-layouts: 2.17 us -> 6.05 us
    psum x1 -> x0, waiting for transfers between devices: 87.1 us -> none  [on_device(): summed_all = lax.psum(partial_sum, 'chol')]
    pallas_call x0 -> x1, Pallas kernels: none -> 82.6 us  [fused(): pl.pallas_call(functools.partial(kernel, n), out_shape=(jax.ShapeDtypeStr...]
    all_gather x1 -> x0, waiting for transfers between devices: 77.7 us -> none  [on_device(): all_rows = lax.all_gather(factor_rows, 'chol', axis=0, tiled=True)]
    dot_general x8 -> x0, matrix products: 47.9 us -> none  [the longest x4 38.9 us: propagate_one(): term = jnp.dot(scaled, all_rows, preferred_element_type=jnp.float32)]
    all_gather x1 -> x0, blocking collectives: 19.5 us -> none  [on_device(): density = lax.all_gather(own_density, 'chol', axis=0, tiled=True)]
    unnamed x9 -> x5, local copies, waits for them, and re-layouts: 1.2 us -> 3.87 us
  transfers between devices with their start and end apart: 2 -> 0, of which waited for: 2 -> 0; matrix products, arithmetic and copies ran while one was open for 1% -> 0% of each run, Pallas kernels for 0% -> 0%
where the time goes in v1:
time: 89.5 us; the launch traced here: 89.3 us
  Pallas kernels  82.6 us (92%)
  local copies, waits for them, and re-layouts  6.05 us (7%)
    pallas_call x1, Pallas kernels, fused(): pl.pallas_call(functools.partial(kernel, n), out_shape=(jax.ShapeDtypeStr...  82.6 us
    unnamed x5, local copies, waits for them, and re-layouts  3.87 us
    pallas_call x1, local copies, waits for them, and re-layouts, fused(): pl.pallas_call(functools.partial(kernel, n), out_shape=(jax.ShapeDtypeStr...  2.19 us

profile of v1, /device:TPU:0, one launch (start us, length us, event | category | flops | bytes accessed | tf_op | source)
XLA Modules:
  0.0 89.3 jit_solution(9929044414124595754)
XLA Ops:
  0.6 1.4 %copy.9.inv_ref = f32[1,100,100]{2,1,0:T(8,128)} copy(f32[1,100,100]{2,0,1:T(1,128)} %param.7) | data formatting | bytes 80000 | tf_op args[1]
  2.1 1.8 %copy.8.orb_ref = f32[1,100,1024]{2,1,0:T(8,128)} copy(f32[1,100,1024]{2,0,1:T(1,128)} %param.6) | data formatting | bytes 819200 | tf_op args[0]
  3.9 82.6 %shard_map.77 = (f32[1,100,1024]{2,1,0:T(8,128)}, f32[16,64]{1,0:T(8,128)}) custom-call(f32[1,100,1024]{2,1,0:T(8,128)} %copy.8.orb_ref, f32[1,100,100]{2,1,0:T(8,128)} %copy.9.inv_ref, bf16[256,1024]{1,0:T(8,128)(2,1)} %rows_ref.1, bf16[100,4096]{1,0:T(8,128)(2,1)} %rot_ref.1, bf16[64,4096]{1,0:T(8,128)(2,1)} %core_ref.1, f32[16,64]{1,0:T(8,128)} %fields_ref.1), custom_call_target="tpu_custom_call" | custom-call | tf_op jit(solution)/shard_map/pallas_call | solution.py:212
  86.5 0.0 copy-start
  86.5 2.2 %copy.10 = f32[1,100,1024]{2,0,1:T(1,128)} copy(f32[1,100,1024]{2,1,0:T(8,128)} %get-tuple-element.2) | data formatting | bytes 819200 | tf_op jit(solution)/shard_map/pallas_call | solution.py:212
  88.7 0.0 copy-done
  88.7 0.6 copy.12
Async XLA Ops:
  86.5 2.2 %copy-start = (f32[16,64]{1,0:T(8,128)S(1)}, f32[16,64]{1,0:T(8,128)}, u32[]{:S(2)}) copy-start(f32[16,64]{1,0:T(8,128)} %get-tuple-element.7) | copy-start | bytes 12292

commit v2 on v1

--- a/solution.py
+++ b/solution.py
@@ -14,16 +14,19 @@
 
 def kernel(
     n, orb_ref, inv_ref, rows_ref, rot_ref, core_ref, fields_ref, out_ref, fb_ref,
-    xbuf, lhs, pad, rot, corep, s1, sc, dbuf, dfull, pbuf, rbuf, pot, tpart, tsend, trecv, tbf, total,
-    own_sem, rot_sem, core_sem, ring_send, ring_recv, pair_send, pair_recv,
-    dens_send, dens_recv, pot_send, pot_recv, term_send, term_recv,
+    xbuf, orb3, lhs, pad, rot, corep, s1, sc, dbuf, dfull, pbuf, rbuf, pot, tpart, tsend, trecv, tbf, total,
+    orb_sem, own_sem, rot_sem, core_sem, ring_send, ring_recv, twin_send, twin_recv, pair_send, pair_recv,
+    dens_send, dens_recv, ready_sem, pot_send, pot_recv, term_send, term_recv,
 ):
     h = n // 2
     p, m = rows_ref.shape
-    ne = orb_ref.shape[1]
+    ne = orb_ref.shape[0]
     nep = pad.shape[0]
     half = h * p
-    piece = p // 2
+    side_rows = p * 5 // 256 * 16
+    sizes = (side_rows, p - 2 * side_rows)
+    here = lax.axis_index("parts")
+    starts = (here * side_rows, 2 * side_rows)
     me = lax.axis_index("chol")
     q, c = me // 2, me % 2
     partner = q * 2 + (1 - c)
@@ -35,9 +38,12 @@
         return (1 - s) * 2 * pos + s * (2 * (h - 1 - pos) + 1)
 
     barrier = pltpu.get_barrier_semaphore()
-    for k in range(1, n):
-        pl.semaphore_signal(barrier, inc=1, device_id={"chol": (me + k) % n}, device_id_type=pl.DeviceIdType.MESH)
-
+    for near in (partner, chip_at(r + 1) * 2 + c, chip_at(r - 1) * 2 + c):
+        pl.semaphore_signal(barrier, inc=1, device_id={"chol": near}, device_id_type=pl.DeviceIdType.MESH)
+    pl.semaphore_signal(barrier, inc=1, device_id={"parts": 1 - here}, device_id_type=pl.DeviceIdType.MESH)
+
+    orb_copy = pltpu.make_async_copy(orb_ref, orb3, orb_sem)
+    orb_copy.start()
     own_copy = pltpu.make_async_copy(rows_ref, xbuf.at[pl.ds(pl.multiple_of(q * p, p), p)], own_sem)
     own_copy.start()
     rot_copy = pltpu.make_async_copy(rot_ref, rot, rot_sem)
@@ -52,7 +58,7 @@
         copy.start()
         core_copies.append(copy)
 
-    pl.semaphore_wait(barrier, n - 1)
+    pl.semaphore_wait(barrier, 4)
 
     def remote(src, dst, send, recv, target):
         return pltpu.make_async_remote_copy(
@@ -60,42 +66,55 @@
             device_id={"chol": target}, device_id_type=pl.DeviceIdType.MESH,
         )
 
-    def slot(chip, part):
-        return xbuf.at[pl.ds(pl.multiple_of(chip * p + part * piece, piece), piece)]
+    def rows(way, step, part):
+        if step < h // 2:
+            return pl.multiple_of(starts[part], 16), sizes[part]
+        if part == 1:
+            return 2 * side_rows + way * (sizes[1] // 2), sizes[1] // 2
+        return pl.multiple_of((way + (1 - 2 * way) * here) * side_rows, 16), side_rows
+
+    def slot(chip, way, step, part):
+        first, size = rows(way, step, part)
+        return xbuf.at[pl.ds(pl.multiple_of(chip * p + first, 16), size)]
+
+    def twin(way, step, row):
+        view = xbuf.at[pl.ds(pl.multiple_of(chip_at(r - (1 - 2 * way) * step) * p + row, 16), side_rows)]
+        return pltpu.make_async_remote_copy(
+            src_ref=view, dst_ref=view, send_sem=twin_send.at[way, step - 1], recv_sem=twin_recv.at[way, step - 1],
+            device_id={"parts": 1 - here}, device_id_type=pl.DeviceIdType.MESH,
+        )
 
     def hop(way, step, part):
         sign = 1 - 2 * way
         origin = chip_at(r - sign * (step - 1))
-        src = rows_ref.at[pl.ds(part * piece, piece)] if step == 1 else slot(origin, part)
+        src = rows_ref.at[pl.ds(*rows(way, step, part))] if step == 1 else slot(origin, way, step, part)
         return remote(
-            src, slot(origin, part), ring_send.at[way, step - 1, part], ring_recv.at[way, step - 1, part],
+            src, slot(origin, way, step, part), ring_send.at[way, step - 1, part], ring_recv.at[way, step - 1, part],
             chip_at(r + sign) * 2 + c,
         )
 
     def arrival(way, step, part):
         sign = 1 - 2 * way
-        here = slot(chip_at(r - sign * step), part)
+        landed = slot(chip_at(r - sign * step), way, step, part)
         return remote(
-            here, here, ring_send.at[way, step - 1, part], ring_recv.at[way, step - 1, part], chip_at(r + sign) * 2 + c
-        )
-
-    def travels(way, step, part):
-        return step < h // 2 or (step == h // 2 and part == way)
+            landed, landed, ring_send.at[way, step - 1, part], ring_recv.at[way, step - 1, part],
+            chip_at(r + sign) * 2 + c,
+        )
 
     sent = []
     for part in range(2):
         for way in range(2):
-            if travels(way, 1, part):
-                copy = hop(way, 1, part)
-                copy.start()
-                sent.append(copy)
-
-    own_walker = orb_ref[0]
+            copy = hop(way, 1, part)
+            copy.start()
+            sent.append(copy)
+
     pad[...] = jnp.zeros_like(pad)
-    pad[0:ne] = own_walker
+    orb_copy.wait()
+    for j in range(m // 128):
+        pad[0:ne, j * 128 : (j + 1) * 128] = orb3[:, j]
     total[...] = pad[...]
     lhs[c, nep : 2 * nep] = pad[...].astype(BF16)
-    pad[0:ne] = jnp.dot(inv_ref[0], own_walker, preferred_element_type=F32, precision=lax.Precision.HIGHEST)
+    pad[0:ne] = jnp.dot(inv_ref[0], pad[0:ne], preferred_element_type=F32, precision=lax.Precision.HIGHEST)
     lhs[c, 0:nep] = pad[...].astype(BF16)
     pair = remote(lhs.at[c], lhs.at[c], pair_send, pair_recv, partner)
     pair.start()
@@ -104,7 +123,7 @@
     rot_copy.wait()
     remote(lhs.at[1 - c], lhs.at[1 - c], pair_send, pair_recv, partner).wait_recv()
 
-    def block(chip):
+    def block(chip, place):
         where = pl.ds(pl.multiple_of(chip * p, p), p)
         result = lax.dot_general(
             lhs[...].reshape(4 * nep, m), xbuf[where, :], LAST, preferred_element_type=F32
@@ -113,34 +132,69 @@
         for w in range(2):
             projected = result[w * 2 * nep : w * 2 * nep + ne]
             density = jnp.sum(rotated * projected, axis=0, keepdims=True)
-            dbuf[me, w : w + 1, where] = density.astype(BF16).astype(F32)
+            dbuf[me, w : w + 1, place * p : (place + 1) * p] = density.astype(BF16).astype(F32)
             s1[w * nep : (w + 1) * nep, where] = result[w * 2 * nep + nep : (w + 1) * 2 * nep]
 
-    block(q)
+    def finish(step):
+        if step < h // 2:
+            for way in range(2 if step < h // 2 - 1 else 1):
+                twin(way, step, (1 - here) * side_rows).wait_recv()
+            block(chip_at(r - step), 2 * step - 1)
+            block(chip_at(r + step), 2 * step)
+        else:
+            block(chip_at(r - step), h - 1)
+
+    cut = (h - 1) * p
+    spans = (pl.ds(0, cut), pl.ds(cut, p))
+
+    def spread(group):
+        for k in range(1, n):
+            view = dbuf.at[me, :, spans[group]]
+            copy = remote(view, view, dens_send.at[group, k - 1], dens_recv.at[group, k - 1], (me + k) % n)
+            copy.start()
+            sent.append(copy)
+
+    block(q, 0)
     for step in range(1, h // 2 + 1):
         for part in range(2):
-            for way in range(2):
-                if travels(way, step, part):
-                    arrival(way, step, part).wait_recv()
-                    if travels(way, step + 1, part):
-                        copy = hop(way, step + 1, part)
-                        copy.start()
-                        sent.append(copy)
-        block(chip_at(r - step))
-        if step < h // 2:
-            block(chip_at(r + step))
-
-    for k in range(1, n):
-        copy = remote(dbuf.at[me], dbuf.at[me], dens_send.at[k - 1], dens_recv.at[k - 1], (me + k) % n)
-        copy.start()
-        sent.append(copy)
+            for way in (1, 0):
+                arrival(way, step, part).wait_recv()
+                if step < h // 2 - 1 or (step == h // 2 - 1 and (way, part) != (1, 0)):
+                    copy = hop(way, step + 1, part)
+                    copy.start()
+                    sent.append(copy)
+                if part == 0 and step < h // 2:
+                    copy = twin(way, step, here * side_rows)
+                    copy.start()
+                    sent.append(copy)
+        if step == h // 2:
+            pl.semaphore_signal(ready_sem, inc=1, device_id={"chol": partner}, device_id_type=pl.DeviceIdType.MESH)
+        if step > 1:
+            finish(step - 1)
+        if step == h // 2 - 1:
+            twin(1, step, (1 - here) * side_rows).wait_recv()
+            copy = hop(1, step + 1, 0)
+            copy.start()
+            sent.append(copy)
+    pl.semaphore_wait(ready_sem, 1)
+    spread(0)
+    finish(h // 2)
+    spread(1)
     for copy in core_copies:
         copy.wait()
-    for k in range(1, n):
-        source = (me + n - k) % n
-        remote(dbuf.at[source], dbuf.at[source], dens_send.at[k - 1], dens_recv.at[k - 1], source).wait_recv()
+    for group in range(2):
+        for k in range(1, n):
+            source = (me + n - k) % n
+            view = dbuf.at[source, :, spans[group]]
+            remote(view, view, dens_send.at[group, k - 1], dens_recv.at[group, k - 1], source).wait_recv()
     for s in range(n):
-        dfull[2 * (s // 2) : 2 * (s // 2) + 2, (s % 2) * half : (s % 2 + 1) * half] = dbuf[s]
+        chip, side = s // 2, s % 2
+        pos = chip // 2 if chip % 2 == 0 else h - 1 - chip // 2
+        for place in range(h):
+            step = (place + 1) // 2
+            other = chip_at(pos - step if place % 2 else pos + step)
+            first = side * half + other * p
+            dfull[2 * chip : 2 * chip + 2, first : first + p] = dbuf[s, :, place * p : (place + 1) * p]
     force_bias = lax.dot_general(dfull[...].astype(BF16), corep[...], LAST, preferred_element_type=F32)
     fb_ref[...] = force_bias
     shifted = (fields_ref[...] - force_bias).astype(BF16)
@@ -193,7 +247,8 @@
             total[:, where] += tpart[j, own] + trecv[order - 1, j, own].astype(F32)
             if not last:
                 tbf[:, where] = (tpart[j] + trecv[order - 1, j].astype(F32)).astype(BF16)
-    out_ref[0] = total[0:ne]
+    for j in range(m // 128):
+        out_ref[:, j] = total[0:ne, j * 128 : (j + 1) * 128]
     for copy in sent:
         copy.wait_send()
 
@@ -209,16 +264,17 @@
     vmem = pl.BlockSpec(memory_space=pltpu.VMEM)
     hbm = pl.BlockSpec(memory_space=pl.ANY)
     dma = pltpu.SemaphoreType.DMA
-    return pl.pallas_call(
+    propagated, force_bias = pl.pallas_call(
         functools.partial(kernel, n),
         out_shape=(
-            jax.ShapeDtypeStruct(orbitals.shape, F32),
+            jax.ShapeDtypeStruct((ne, m // 128, 128), F32),
             jax.ShapeDtypeStruct(fields.shape, F32),
         ),
-        in_specs=[vmem, vmem, hbm, hbm, hbm, vmem],
+        in_specs=[hbm, vmem, hbm, hbm, hbm, vmem],
         out_specs=(vmem, vmem),
         scratch_shapes=[
             pltpu.VMEM((half, m), BF16),
+            pltpu.VMEM((ne, m // 128, 128), F32),
             pltpu.VMEM((2, 2 * nep, m), BF16),
             pltpu.VMEM((nep, m), F32),
             pltpu.VMEM((ne, points), BF16),
@@ -237,13 +293,17 @@
             pltpu.VMEM((nep, m), F32),
             dma(()),
             dma(()),
+            dma(()),
             dma((n,)),
             dma((2, h // 2, 2)),
             dma((2, h // 2, 2)),
-            dma(()),
-            dma(()),
-            dma((n - 1,)),
-            dma((n - 1,)),
+            dma((2, h // 2)),
+            dma((2, h // 2)),
+            dma(()),
+            dma(()),
+            dma((2, n - 1)),
+            dma((2, n - 1)),
+            pltpu.SemaphoreType.REGULAR,
             dma((n - 1,)),
             dma((n - 1,)),
             dma((TAYLOR, m // wide)),
@@ -252,7 +312,8 @@
         compiler_params=pltpu.CompilerParams(
             collective_id=0, has_side_effects=True, vmem_limit_bytes=56 * 1024 * 1024
         ),
-    )(orbitals, intersection_inv, factor_rows, factor_rotated, factor_core, fields)
+    )(orbitals.reshape(ne, m // 128, 128), intersection_inv, factor_rows, factor_rotated, factor_core, fields)
+    return propagated.reshape(orbitals.shape), force_bias
 
 
 def density_one(half_green, all_rows, factor_rotated):
@@ -296,7 +357,7 @@
     def on_device(orbitals, intersection_inv, factor_rows, factor_rotated, factor_core, fields):
         args = (orbitals, intersection_inv, factor_rows, factor_rotated, factor_core, fields)
         rows, m = factor_rows.shape
-        if orbitals.shape[0] == 1 and n % 4 == 0 and rows % 256 == 0 and m % 256 == 0:
+        if orbitals.shape[0] == 1 and n % 4 == 0 and n > 8 and rows % 256 == 0 and mesh.shape["parts"] == 2 and m % 256 == 0:
             return fused(*args, n)
         return plain(*args)
 

time: 89.5 us -> 77.5 us (0.87)
  Pallas kernels: 82.6 us -> 72.6 us
  local copies, waits for them, and re-layouts: 6.05 us -> 3.82 us
    pallas_call x1, Pallas kernels: 82.6 us -> 72.6 us  [fused(): pl.pallas_call(functools.partial(kernel, n), out_shape=(jax.ShapeDtypeStr...]
    pallas_call x1 -> x0, local copies, waits for them, and re-layouts: 2.19 us -> none  [fused(): pl.pallas_call(functools.partial(kernel, n), out_shape=(jax.ShapeDtypeStr...]
where the time goes in v2:
time: 77.5 us; the launch traced here: 77 us
  Pallas kernels  72.6 us (94%)
  local copies, waits for them, and re-layouts  3.82 us (5%)
    pallas_call x1, Pallas kernels, fused(): pl.pallas_call(functools.partial(kernel, n), out_shape=(jax.ShapeDtypeStr...  72.6 us
    unnamed x5, local copies, waits for them, and re-layouts  3.82 us

profile of v2, /device:TPU:0, one launch (start us, length us, event | category | flops | bytes accessed | tf_op | source)
XLA Modules:
  0.0 77.0 jit_solution(15847321237892020530)
XLA Ops:
  0.6 1.4 %copy.10.inv_ref = f32[1,100,100]{2,1,0:T(8,128)} copy(f32[1,100,100]{2,0,1:T(1,128)} %param.7) | data formatting | bytes 80000 | tf_op args[1]
  2.1 72.6 %shard_map.77 = (f32[100,8,128]{2,1,0:T(8,128)}, f32[16,64]{1,0:T(8,128)}) custom-call(f32[100,8,128]{2,1,0:T(8,128)} %bitcast.2, f32[1,100,100]{2,1,0:T(8,128)} %copy.10.inv_ref, bf16[256,1024]{1,0:T(8,128)(2,1)} %rows_ref.1, bf16[100,4096]{1,0:T(8,128)(2,1)} %rot_ref.1, bf16[64,4096]{1,0:T(8,128)(2,1)} %core_ref.1, f32[16,64]{1,0:T(8,128)} %fields_ref.1), custom_call_target="tpu_custom_call" | custom-call | tf_op jit(solution)/shard_map/pallas_call | solution.py:267
  74.7 0.0 copy-start
  74.7 1.8 %copy.14 = f32[1,100,1024]{2,0,1:T(1,128)} copy(f32[1,100,1024]{2,0,1:T(1,128)} %bitcast.3) | data formatting | bytes 819200
  76.4 0.0 copy-done
  76.5 0.6 copy.15
Async XLA Ops:
  74.7 1.8 %copy-start = (f32[16,64]{1,0:T(8,128)S(1)}, f32[16,64]{1,0:T(8,128)}, u32[]{:S(2)}) copy-start(f32[16,64]{1,0:T(8,128)} %get-tuple-element.13) | copy-start | bytes 12292
